TPU v7x, 32 devices: a whole 2x2x4 slice. The times are simulated.
32 devices in a mesh: dom: 2 (over y), frame: 4 (over z), query: 2 (over x), split: 2 (over core).
Axes of the slice: x: 2, y: 2, z: 4, core: 2. Of those that a mesh axis runs over, the one named last changes fastest.
Arguments:
- frames: bfloat16 [16, 1024, 256], P(('dom', 'frame')), parts along dimension 0, may hold values from -64 to 64
- query_frame: int32 [2048], P(('dom', 'query')), parts along dimension 0, may hold values from 0 to 7, as said below
- query_pixel: int32 [2, 2048], P(None, ('dom', 'query')), parts along dimension 1, may hold values from 0 to 31
- in_weight: bfloat16 [512, 512], replicated, may hold values from -0.25 to 0.25
- conv_weight: float32 [1, 3, 512], replicated, may hold values from -3 to 3
- up_weight: bfloat16 [1, 512, 2048], P(None, None, 'split'), may hold values from -0.25 to 0.25
- down_weight: bfloat16 [1, 2048, 512], P(None, 'split'), may hold values from -0.125 to 0.125
Outputs:
- tokens: bfloat16 [2048, 8, 512], P(('dom', 'query'), 'frame'), parts along dimension 0
There are 2 independent parts, one for each index of `dom`. A program takes and returns all parts, laid end to end along the dimension named above; an argument that names none is the same for every part. Nothing has to cross between parts.
Inputs may be any that keep to these rules, and one draw needn't show every extreme that they name: `query_frame`: within each aligned group of 512 query points (one index of query), at most 384 start frames lie among any aligned 2 frames (one index of frame), and in every group some such frames hold exactly 384.
All inputs are finite; a program needn't handle non-finite values.
Results may differ from a plain program's by a relative error of at most 0.006.
Values may be sent and summed in bfloat16 or wider, within the bound.
No kernel may reach another device: no remote copies, remote signals or barrier semaphores. Data moves between devices by JAX's collectives and lax.ppermute only.
A program may use at most 64 MiB of HBM per device.

v0:
```python
import math
import jax
import jax.numpy as jnp
from jax import lax
from jax.sharding import PartitionSpec as P

SIDE = 32


def with_halo(cells, sides, width):
    for axis, dim in sides:
        count = lax.axis_size(axis)
        ends = count - 1
        head = lax.slice_in_dim(cells, 0, width, axis=dim)
        tail = lax.slice_in_dim(cells, cells.shape[dim] - width, cells.shape[dim], axis=dim)
        cells = jnp.concatenate(
            [
                lax.ppermute(tail, axis, [(i, (i + 1) % count) for i in range(ends)]),
                cells,
                lax.ppermute(head, axis, [((i + 1) % count, i) for i in range(ends)]),
            ],
            axis=dim,
        )
    return cells


def rms_scale(values, epsilon):
    return values / jnp.sqrt(jnp.mean(values * values, axis=-1, keepdims=True) + epsilon)


def on_device(frames, query_frame, query_pixel, in_weight, conv_weight, up_weight, down_weight):
    frame_count, pixel_count, channels = frames.shape
    query_count = query_frame.shape[0]
    width = in_weight.shape[1]
    first_frame = lax.axis_index("frame") * frame_count
    flat_frames = frames.reshape(frame_count * pixel_count, channels)
    pixel_index = query_pixel[0] * SIDE + query_pixel[1]
    local_frame = query_frame - first_frame
    is_owned = (local_frame >= 0) & (local_frame < frame_count)
    column = jnp.where(is_owned, local_frame * pixel_count + pixel_index, -1)
    picker = (
        column[:, None] == jnp.arange(frame_count * pixel_count, dtype=jnp.int32)[None, :]
    ).astype(jnp.bfloat16)
    own_features = jnp.dot(picker, flat_frames, preferred_element_type=jnp.float32)
    devices = lax.axis_size("frame")
    capacity = max(2, 3 * query_count // devices)
    owner = query_frame // frame_count
    order = jnp.arange(query_count, dtype=jnp.int32)
    earlier = (owner[:, None] == owner[None, :]) & (order[None, :] < order[:, None])
    ranking = jnp.sum(earlier.astype(jnp.int32), axis=1)
    slot_pick = (
        (ranking[None, :] == jnp.arange(capacity, dtype=jnp.int32)[:, None]) & is_owned[None, :]
    ).astype(jnp.bfloat16)
    packed = jnp.dot(
        slot_pick, own_features.astype(jnp.bfloat16), preferred_element_type=jnp.float32
    ).astype(jnp.bfloat16)
    every_slot = lax.all_gather(packed, "frame", axis=0, tiled=True)
    source = owner * capacity + ranking
    unpick = (source[:, None] == jnp.arange(devices * capacity, dtype=jnp.int32)[None, :]).astype(
        jnp.bfloat16
    )
    query_features = jnp.dot(unpick, every_slot, preferred_element_type=jnp.float32).astype(
        jnp.bfloat16
    )
    scores = jnp.einsum(
        "qc,tpc->qtp", query_features, frames, preferred_element_type=jnp.float32
    ) * (1.0 / math.sqrt(channels))
    peak = jnp.max(scores, axis=-1, keepdims=True)
    expd = jnp.exp(scores - peak)
    weights = (expd / jnp.sum(expd, axis=-1, keepdims=True)).astype(jnp.bfloat16)
    pooled = jnp.einsum("qtp,tpc->qtc", weights, frames, preferred_element_type=jnp.float32)
    normed = rms_scale(pooled, 1e-06).astype(jnp.bfloat16)
    joined = jnp.concatenate(
        [normed, jnp.broadcast_to(query_features[:, None, :], normed.shape)], axis=-1
    )
    stream = jnp.einsum("qtc,cd->qtd", joined, in_weight, preferred_element_type=jnp.float32)
    rows_total = query_count * frame_count
    level = rms_scale(stream, 1e-05).astype(jnp.bfloat16)
    padded = with_halo(level, (("frame", 1),), 1).astype(jnp.float32)
    taps = conv_weight[0]
    mixed_time = taps[0] * padded[:, :-2] + taps[1] * padded[:, 1:-1] + taps[2] * padded[:, 2:]
    stream = stream + mixed_time
    gated = rms_scale(stream, 1e-05).astype(jnp.bfloat16).reshape(rows_total, width)
    hidden = jax.nn.gelu(jnp.dot(gated, up_weight[0], preferred_element_type=jnp.float32)).astype(
        jnp.bfloat16
    )
    partial_delta = jnp.dot(hidden, down_weight[0], preferred_element_type=jnp.float32)
    summed = lax.psum(partial_delta.astype(jnp.bfloat16), "split").astype(jnp.float32)
    stream = stream + summed.reshape(query_count, frame_count, width)
    return stream.astype(jnp.bfloat16)


def solution(mesh):
    return jax.shard_map(
        on_device,
        mesh=mesh,
        in_specs=(
            P(("dom", "frame"), None, None),
            P(("dom", "query")),
            P(None, ("dom", "query")),
            P(),
            P(),
            P(None, None, "split"),
            P(None, "split", None),
        ),
        out_specs=P(("dom", "query"), "frame", None),
        check_vma=False,
    )
```

profile of v0, /device:TPU:0, one launch (start us, length us, event | category | flops | bytes accessed | tf_op | source)
XLA Modules:
  0.0 102.2 jit_solution(10552802000820765589)
XLA Ops:
  6.5 0.8 slice_add_fusion
  7.3 0.7 compare_and_fusion
  8.0 0.7 add_select_fusion
  9.0 1.2 %convolution_convert_fusion.1 = bf16[384,256]{1,0:T(8,128)(2,1)S(1)} fusion(bf16[2048,256]{1,0:T(8,128)(2,1)S(1)} %bitcast.38, s32[512]{0:T(512)S(1)} %get-tuple-element.13, s32[512]{0:T(512)S(1)} %convert_reduce_fusion, pred[512]{0:T(512)(128)(4,1)S(1)} %compare_and_fusion), kind=kOutput, calls=%fused_computation.38 | convolution fusion | flops 639205376 | bytes 1249792 | tf_op jit(solution)/shard_map/dot_general | solution.py:54
  10.2 21.3 %all_gather.3 = bf16[1536,256]{1,0:T(8,128)(2,1)S(1)} all-gather(bf16[384,256]{1,0:T(8,128)(2,1)S(1)} %convolution_convert_fusion.1), channel_id=1, replica_groups=mesh['dom'=2,'frame'=4,'query'=2,'split'=2] {'frame'}, dimensions={0}, use_global_device_ids=true | all-gather | bytes 983040 | tf_op jit(solution)/shard_map/all_gather | solution.py:57
  31.5 0.7 fusion.23
  32.3 3.3 %fusion.57 = (f32[512,2]{0,1:T(2,128)S(1)}, f32[512,2,1024]{2,0,1:T(8,128)}) fusion(bf16[2,1024,256]{2,1,0:T(8,128)(2,1)S(1)} %copy-done, bf16[512,256]{1,0:T(8,128)(2,1)S(1)} %fusion.23), kind=kOutput, calls=%fused_computation.81 | convolution fusion | flops 540017664 | bytes 5509120 | tf_op jit(solution)/shard_map/sub | solution.py:69
  35.6 3.1 %multiply_reduce_fusion.3 = (f32[512,2]{0,1:T(2,128)S(1)}, f32[512,2,256]{0,2,1:T(8,128)S(1)}) fusion(bf16[2,1024,256]{2,1,0:T(8,128)(2,1)S(1)} %copy-done, f32[512,2,1024]{2,0,1:T(8,128)} %get-tuple-element.15, f32[512,2]{0,1:T(2,128)S(1)} %get-tuple-element.14), kind=kOutput, calls=%fused_computation.46 | convolution fusion | flops 539491328 | bytes 6299648 | tf_op jit(solution)/shard_map/qtp,tpc->qtc/dot_general | solution.py:71
  38.9 0.8 copy-done.2
  39.7 0.8 multiply_reduce_fusion.2
  40.9 1.6 %collective-permute-start = (bf16[512,1,512]{2,0,1:T(8,128)(2,1)S(1)}, bf16[512,1,512]{2,0,1:T(8,128)(2,1)S(1)}, u32[]{:S(2)}, u32[]{:S(2)}) collective-permute-start(bf16[512,1,512]{2,0,1:T(8,128)(2,1)S(1)} %get-tuple-element.7), channel_id=1, source_target_pairs={{0,4},{4,8},{8,12},{1,5},{5,9},{9,13},{2,6},{6,10},{10,14},{3,7},{... | collective-permute-start | bytes 1572872 | tf_op jit(solution)/shard_map/ppermute | solution.py:18
  42.4 1.5 %collective-permute-start.1 = (bf16[512,1,512]{2,0,1:T(8,128)(2,1)S(1)}, bf16[512,1,512]{2,0,1:T(8,128)(2,1)S(1)}, u32[]{:S(2)}, u32[]{:S(2)}) collective-permute-start(bf16[512,1,512]{2,0,1:T(8,128)(2,1)S(1)} %get-tuple-element.8), channel_id=1, source_target_pairs={{4,0},{8,4},{12,8},{5,1},{9,5},{13,9},{6,2},{10,6},{14,10},{7,3},{... | collective-permute-start | bytes 1572872 | tf_op jit(solution)/shard_map/ppermute | solution.py:20
  43.9 8.1 %collective-permute-done = bf16[512,1,512]{2,0,1:T(8,128)(2,1)S(1)} collective-permute-done((bf16[512,1,512]{2,0,1:T(8,128)(2,1)S(1)}, bf16[512,1,512]{2,0,1:T(8,128)(2,1)S(1)}, u32[]{:S(2)}, u32[]{:S(2)}) %collective-permute-start) | collective-permute-done | bytes 524320 | tf_op jit(solution)/shard_map/ppermute | solution.py:18
  52.0 4.1 %collective-permute-done.1 = bf16[512,1,512]{2,0,1:T(8,128)(2,1)S(1)} collective-permute-done((bf16[512,1,512]{2,0,1:T(8,128)(2,1)S(1)}, bf16[512,1,512]{2,0,1:T(8,128)(2,1)S(1)}, u32[]{:S(2)}, u32[]{:S(2)}) %collective-permute-start.1) | collective-permute-done | bytes 524320 | tf_op jit(solution)/shard_map/ppermute | solution.py:20
  56.2 0.3 maximum_convert_fusion
  56.5 0.7 multiply_reduce_fusion.1
  57.4 2.0 %copy.21 = bf16[512,2,512]{2,1,0:T(2,128)(2,1)} copy(bf16[512,2,512]{2,0,1:T(8,128)(2,1)S(1)} %divide_convert_fusion.1) | data formatting | bytes 2097152 | tf_op jit(solution)/shard_map/convert_element_type | solution.py:83
  59.5 2.3 %reshape.55 = bf16[1024,512]{1,0:T(8,128)(2,1)} reshape(bf16[512,2,512]{2,1,0:T(2,128)(2,1)} %copy.21) | data formatting | bytes 2097152 | tf_op jit(solution)/shard_map/reshape | solution.py:83
  61.7 5.2 %convolution_convert_fusion = bf16[1024,512]{1,0:T(8,128)(2,1)} fusion(bf16[1024,512]{1,0:T(8,128)(2,1)} %reshape.55, bf16[1,1024,512]{2,1,0:T(8,128)(2,1)} %param.13, bf16[1,512,1024]{2,1,0:T(8,128)(2,1)} %param.12), kind=kOutput, calls=%fused_computation.34 | convolution fusion | flops 2157445120 | bytes 4194304 | tf_op jit(solution)/shard_map/dot_general | solution.py:87
  67.0 2.3 %reshape.56 = bf16[512,2,512]{2,1,0:T(2,128)(2,1)} reshape(bf16[1024,512]{1,0:T(8,128)(2,1)} %convolution_convert_fusion) | data formatting | bytes 2097152 | tf_op jit(solution)/shard_map/reshape | solution.py:89
  69.2 2.4 %copy.22 = bf16[512,2,512]{2,0,1:T(8,128)(2,1)} copy(bf16[512,2,512]{2,1,0:T(2,128)(2,1)} %reshape.56) | data formatting | bytes 2097152 | tf_op jit(solution)/shard_map/reshape | solution.py:89
  71.6 20.1 %all-reduce.2.cloned.1.call-done = bf16[512,2,512]{2,0,1:T(8,128)(2,1)} async-done(((bf16[512,2,512]{2,0,1:T(8,128)(2,1)}), bf16[512,2,512]{2,0,1:T(8,128)(2,1)}) %all-reduce.2.cloned.1.call-update) | async-done | bytes 1048592 | tf_op jit(solution)/shard_map/psum | solution.py:88
  91.7 1.6 %add_convert_fusion = bf16[512,2,512]{2,0,1:T(8,128)(2,1)S(1)} fusion(f32[512,2,512]{2,0,1:T(8,128)S(1)} %get-tuple-element.6, bf16[512,2,512]{2,0,1:T(8,128)(2,1)} %all-reduce.2.cloned.1.call-done), kind=kLoop, calls=%fused_computation.25 | loop fusion | flops 1572864 | bytes 4194304 | tf_op jit(solution)/shard_map/convert_element_type | solution.py:90
  93.3 2.0 %copy.23 = bf16[512,2,512]{2,1,0:T(2,128)(2,1)} copy(bf16[512,2,512]{2,0,1:T(8,128)(2,1)S(1)} %add_convert_fusion) | data formatting | bytes 2097152 | tf_op jit(solution)/shard_map/convert_element_type | solution.py:90
  (19 shorter events, 1.1 us)
Async XLA Ops:
  6.5 2.4 %copy-start = (bf16[2,1024,256]{2,1,0:T(8,128)(2,1)S(1)}, bf16[2,1024,256]{2,1,0:T(8,128)(2,1)}, u32[]{:S(2)}) copy-start(bf16[2,1024,256]{2,1,0:T(8,128)(2,1)} %param.7) | copy-start | bytes 3145732
  6.5 85.2 %all-reduce.2.cloned.1.call-start = ((), (), s32[]{:S(2)}) async-start(), calls=%async_computation | async-start | bytes 2097152 | tf_op jit(solution)/shard_map/psum | solution.py:88
  38.7 1.0 %copy-start.2 = (bf16[512,512]{1,0:T(8,128)(2,1)S(1)}, bf16[512,512]{1,0:T(8,128)(2,1)}, u32[]{:S(2)}) copy-start(bf16[512,512]{1,0:T(8,128)(2,1)} %param.10) | copy-start | bytes 1572868
  40.6 3.4 %copy-start.1 = (f32[1,3,512]{2,0,1:T(1,128)S(1)}, f32[1,3,512]{2,0,1:T(1,128)}, u32[]{:S(2)}) copy-start(f32[1,3,512]{2,0,1:T(1,128)} %param.11) | copy-start | bytes 18436
  40.9 11.2 %collective-permute-start = (bf16[512,1,512]{2,0,1:T(8,128)(2,1)S(1)}, bf16[512,1,512]{2,0,1:T(8,128)(2,1)S(1)}, u32[]{:S(2)}, u32[]{:S(2)}) collective-permute-start(bf16[512,1,512]{2,0,1:T(8,128)(2,1)S(1)} %get-tuple-element.7), channel_id=1, source_target_pairs={{0,4},{4,8},{8,12},{1,5},{5,9},{9,13},{2,6},{6,10},{10,14},{3,7},{... | collective-permute-start | bytes 1572872 | tf_op jit(solution)/shard_map/ppermute | solution.py:18
  42.4 13.7 %collective-permute-start.1 = (bf16[512,1,512]{2,0,1:T(8,128)(2,1)S(1)}, bf16[512,1,512]{2,0,1:T(8,128)(2,1)S(1)}, u32[]{:S(2)}, u32[]{:S(2)}) collective-permute-start(bf16[512,1,512]{2,0,1:T(8,128)(2,1)S(1)} %get-tuple-element.8), channel_id=1, source_target_pairs={{4,0},{8,4},{12,8},{5,1},{9,5},{13,9},{6,2},{10,6},{14,10},{7,3},{... | collective-permute-start | bytes 1572872 | tf_op jit(solution)/shard_map/ppermute | solution.py:20
Sparse Core Ops, SparseCore 0:
  71.7 19.9 all-reduce.1
where the time goes:
time: 103 us; the launch traced here: 102 us
  waiting for transfers between devices  32.4 us (31%)
  blocking collectives  21.3 us (21%)
  matrix products  14.3 us (14%)
  between operations  13.5 us (13%)
  local copies, waits for them, and re-layouts  12.1 us (12%)
  other arithmetic  5.59 us (5%)
  starting transfers between devices  3.05 us (3%)
    all_gather x1, blocking collectives, on_device(): every_slot = lax.all_gather(packed, 'frame', axis=0, tiled=True)  21.3 us
    psum x1, waiting for transfers between devices, on_device(): lax.psum(partial_delta.astype(jnp.bfloat16), 'split').astype(jnp.float32)  20.1 us
    ppermute x1, waiting for transfers between devices, with_halo(): lax.ppermute(tail, axis, [(i, (i + 1) % count) for i in range(ends)])  8.08 us
    dot_general x1, matrix products, on_device(): jnp.dot(hidden, down_weight[0], preferred_element_type=jnp.float32)  5.25 us
    reshape x2, local copies, waits for them, and re-layouts, on_device(): stream = stream + summed.reshape(query_count, frame_count, width)  4.62 us
    ppermute x1, waiting for transfers between devices, with_halo(): lax.ppermute(head, axis, [((i + 1) % count, i) for i in range(ends)])  4.15 us
    sub x1, matrix products, on_device(): expd = jnp.exp(scores - peak)  3.28 us
    dot_general x1, matrix products, on_device(): jnp.einsum('qtp,tpc->qtc', weights, frames, preferred_element_type=jnp.fl...  3.07 us
  transfers between devices with their start and end apart: 3, of which 3 were waited for; matrix products, arithmetic and copies ran while one was open for 0% of the time, Pallas kernels for 0%

commit v1 on v0

--- a/solution.py
+++ b/solution.py
@@ -5,6 +5,24 @@
 from jax.sharding import PartitionSpec as P
 
 SIDE = 32
+
+
+def laid_out(blocks, dim):
+    blocks = jnp.moveaxis(blocks, 0, dim)
+    shape = blocks.shape
+    return blocks.reshape(*shape[:dim], shape[dim] * shape[dim + 1], *shape[dim + 2 :])
+
+
+def grow_blocks(x, axis):
+    count = lax.axis_size(axis)
+    blocks = x[None]
+    for level in range(count.bit_length() - 1):
+        bit = 1 << level
+        received = lax.ppermute(blocks, axis, [(i, i ^ bit) for i in range(count)])
+        both = jnp.stack([blocks, received])
+        upper = lax.axis_index(axis) >> level & 1
+        blocks = jnp.where(upper == 0, both, both[::-1]).reshape(-1, *x.shape)
+    return blocks
 
 
 def with_halo(cells, sides, width):
@@ -54,7 +72,7 @@
     packed = jnp.dot(
         slot_pick, own_features.astype(jnp.bfloat16), preferred_element_type=jnp.float32
     ).astype(jnp.bfloat16)
-    every_slot = lax.all_gather(packed, "frame", axis=0, tiled=True)
+    every_slot = laid_out(grow_blocks(packed, "frame"), 0)
     source = owner * capacity + ranking
     unpick = (source[:, None] == jnp.arange(devices * capacity, dtype=jnp.int32)[None, :]).astype(
         jnp.bfloat16

time: 103 us -> 112 us (1.087)
  waiting for transfers between devices: 32.4 us -> 56.3 us
  blocking collectives: 21.3 us -> 0 us
  starting transfers between devices: 3.05 us -> 9.91 us
    ppermute x0 -> x2, waiting for transfers between devices: none -> 21.7 us  [grow_blocks(): received = lax.ppermute(blocks, axis, [(i, i ^ bit) for i in range(count)])]
    all_gather x1 -> x0, blocking collectives: 21.3 us -> none  [on_device(): every_slot = lax.all_gather(packed, 'frame', axis=0, tiled=True)]
    ppermute x0 -> x2, starting transfers between devices: none -> 5.94 us  [grow_blocks(): received = lax.ppermute(blocks, axis, [(i, i ^ bit) for i in range(count)])]
    ppermute x1, waiting for transfers between devices: 8.08 us -> 9.81 us  [with_halo(): lax.ppermute(tail, axis, [(i, (i + 1) % count) for i in range(ends)])]
  transfers between devices with their start and end apart: 3 -> 5, of which waited for: 3 -> 5; matrix products, arithmetic and copies ran while one was open for 0% -> 0% of each run, Pallas kernels for 0% -> 0%
where the time goes in v1:
time: 112 us
  waiting for transfers between devices  56.3 us (50%)
  matrix products  14.3 us (13%)
  between operations  13.6 us (12%)
  local copies, waits for them, and re-layouts  12.1 us (11%)
  starting transfers between devices  9.91 us (9%)
  other arithmetic  5.94 us (5%)
    ppermute x2, waiting for transfers between devices, grow_blocks(): received = lax.ppermute(blocks, axis, [(i, i ^ bit) for i in range(count)])  21.7 us
    psum x1, waiting for transfers between devices, on_device(): lax.psum(partial_delta.astype(jnp.bfloat16), 'split').astype(jnp.float32)  20.6 us
    ppermute x1, waiting for transfers between devices, with_halo(): lax.ppermute(tail, axis, [(i, (i + 1) % count) for i in range(ends)])  9.81 us
    ppermute x2, starting transfers between devices, grow_blocks(): received = lax.ppermute(blocks, axis, [(i, i ^ bit) for i in range(count)])  5.94 us
    dot_general x1, matrix products, on_device(): jnp.dot(hidden, down_weight[0], preferred_element_type=jnp.float32)  5.25 us
    reshape x2, local copies, waits for them, and re-layouts, on_device(): stream = stream + summed.reshape(query_count, frame_count, width)  4.62 us
    ppermute x1, waiting for transfers between devices, with_halo(): lax.ppermute(head, axis, [((i + 1) % count, i) for i in range(ends)])  4.15 us
    sub x1, matrix products, on_device(): expd = jnp.exp(scores - peak)  3.28 us
  transfers between devices with their start and end apart: 5, of which 5 were waited for; matrix products, arithmetic and copies ran while one was open for 0% of the time, Pallas kernels for 0%

profile of v1, /device:TPU:0, one launch (start us, length us, event | category | flops | bytes accessed | tf_op | source)
XLA Modules:
  0.0 112.1 jit_solution(4409674771107431858)
XLA Ops:
  6.5 0.8 slice_add_fusion
  7.3 0.7 compare_and_fusion
  8.0 0.7 add_select_fusion
  9.0 1.2 %convolution_convert_fusion.1 = bf16[384,256]{1,0:T(8,128)(2,1)S(1)} fusion(bf16[2048,256]{1,0:T(8,128)(2,1)S(1)} %bitcast.47, s32[512]{0:T(512)S(1)} %get-tuple-element.15, s32[512]{0:T(512)S(1)} %convert_reduce_fusion, pred[512]{0:T(512)(128)(4,1)S(1)} %compare_and_fusion), kind=kOutput, calls=%fused_computation.39 | convolution fusion | flops 639205376 | bytes 1249792 | tf_op jit(solution)/shard_map/dot_general | solution.py:72
  10.2 3.1 %collective-permute-start = (bf16[1,384,256]{2,1,0:T(8,128)(2,1)S(1)}, bf16[1,384,256]{2,1,0:T(8,128)(2,1)S(1)}, u32[]{:S(2)}, u32[]{:S(2)}) collective-permute-start(bf16[1,384,256]{2,1,0:T(8,128)(2,1)S(1)} %bitcast.50), channel_id=1, source_target_pairs={{0,4},{4,0},{8,12},{12,8},{1,5},{5,1},{9,13},{13,9},{2,6},{6,2},{1... | collective-permute-start | bytes 589832 | tf_op jit(solution)/shard_map/ppermute | solution.py:21
  13.3 4.9 %collective-permute-done = bf16[1,384,256]{2,1,0:T(8,128)(2,1)S(1)} collective-permute-done((bf16[1,384,256]{2,1,0:T(8,128)(2,1)S(1)}, bf16[1,384,256]{2,1,0:T(8,128)(2,1)S(1)}, u32[]{:S(2)}, u32[]{:S(2)}) %collective-permute-start) | collective-permute-done | bytes 196640 | tf_op jit(solution)/shard_map/ppermute | solution.py:21
  18.3 2.8 %collective-permute-start.1 = (bf16[2,384,256]{2,1,0:T(8,128)(2,1)S(1)}, bf16[2,384,256]{2,1,0:T(8,128)(2,1)S(1)}, u32[]{:S(2)}, u32[]{:S(2)}) collective-permute-start(bf16[2,384,256]{2,1,0:T(8,128)(2,1)S(1)} %get-tuple-element.10), channel_id=1, source_target_pairs={{0,8},{4,12},{8,0},{12,4},{1,9},{5,13},{9,1},{13,5},{2,10},{6,14},... | collective-permute-start | bytes 1179656 | tf_op jit(solution)/shard_map/ppermute | solution.py:21
  21.1 16.8 %collective-permute-done.1 = bf16[2,384,256]{2,1,0:T(8,128)(2,1)S(1)} collective-permute-done((bf16[2,384,256]{2,1,0:T(8,128)(2,1)S(1)}, bf16[2,384,256]{2,1,0:T(8,128)(2,1)S(1)}, u32[]{:S(2)}, u32[]{:S(2)}) %collective-permute-start.1) | collective-permute-done | bytes 393248 | tf_op jit(solution)/shard_map/ppermute | solution.py:21
  39.0 3.3 %fusion.59 = (f32[512,2]{0,1:T(2,128)S(1)}, f32[512,2,1024]{2,0,1:T(8,128)}) fusion(bf16[2,1024,256]{2,1,0:T(8,128)(2,1)S(1)} %copy-done, bf16[512,256]{1,0:T(8,128)(2,1)S(1)} %fusion.23), kind=kOutput, calls=%fused_computation.87 | convolution fusion | flops 540017664 | bytes 5509120 | tf_op jit(solution)/shard_map/sub | solution.py:87
  42.3 3.1 %multiply_reduce_fusion.3 = (f32[512,2]{0,1:T(2,128)S(1)}, f32[512,2,256]{0,2,1:T(8,128)S(1)}) fusion(bf16[2,1024,256]{2,1,0:T(8,128)(2,1)S(1)} %copy-done, f32[512,2,1024]{2,0,1:T(8,128)} %get-tuple-element.17, f32[512,2]{0,1:T(2,128)S(1)} %get-tuple-element.16), kind=kOutput, calls=%fused_computation.47 | convolution fusion | flops 539491328 | bytes 6299648 | tf_op jit(solution)/shard_map/qtp,tpc->qtc/dot_general | solution.py:89
  45.6 0.8 copy-done.2
  46.4 0.8 multiply_reduce_fusion.2
  47.6 2.5 %collective-permute-start.2 = (bf16[512,1,512]{2,0,1:T(8,128)(2,1)S(1)}, bf16[512,1,512]{2,0,1:T(8,128)(2,1)S(1)}, u32[]{:S(2)}, u32[]{:S(2)}) collective-permute-start(bf16[512,1,512]{2,0,1:T(8,128)(2,1)S(1)} %get-tuple-element.7), channel_id=1, source_target_pairs={{0,4},{4,8},{8,12},{1,5},{5,9},{9,13},{2,6},{6,10},{10,14},{3,7},{... | collective-permute-start | bytes 1572872 | tf_op jit(solution)/shard_map/ppermute | solution.py:36
  50.1 1.5 %collective-permute-start.3 = (bf16[512,1,512]{2,0,1:T(8,128)(2,1)S(1)}, bf16[512,1,512]{2,0,1:T(8,128)(2,1)S(1)}, u32[]{:S(2)}, u32[]{:S(2)}) collective-permute-start(bf16[512,1,512]{2,0,1:T(8,128)(2,1)S(1)} %get-tuple-element.8), channel_id=1, source_target_pairs={{4,0},{8,4},{12,8},{5,1},{9,5},{13,9},{6,2},{10,6},{14,10},{7,3},{... | collective-permute-start | bytes 1572872 | tf_op jit(solution)/shard_map/ppermute | solution.py:38
  51.6 9.8 %collective-permute-done.2 = bf16[512,1,512]{2,0,1:T(8,128)(2,1)S(1)} collective-permute-done((bf16[512,1,512]{2,0,1:T(8,128)(2,1)S(1)}, bf16[512,1,512]{2,0,1:T(8,128)(2,1)S(1)}, u32[]{:S(2)}, u32[]{:S(2)}) %collective-permute-start.2) | collective-permute-done | bytes 524320 | tf_op jit(solution)/shard_map/ppermute | solution.py:36
  61.4 4.1 %collective-permute-done.3 = bf16[512,1,512]{2,0,1:T(8,128)(2,1)S(1)} collective-permute-done((bf16[512,1,512]{2,0,1:T(8,128)(2,1)S(1)}, bf16[512,1,512]{2,0,1:T(8,128)(2,1)S(1)}, u32[]{:S(2)}, u32[]{:S(2)}) %collective-permute-start.3) | collective-permute-done | bytes 524320 | tf_op jit(solution)/shard_map/ppermute | solution.py:38
  66.8 2.0 %copy.21 = bf16[512,2,512]{2,1,0:T(2,128)(2,1)} copy(bf16[512,2,512]{2,0,1:T(8,128)(2,1)S(1)} %divide_convert_fusion.1) | data formatting | bytes 2097152 | tf_op jit(solution)/shard_map/convert_element_type | solution.py:101
  68.9 2.3 %reshape.59 = bf16[1024,512]{1,0:T(8,128)(2,1)} reshape(bf16[512,2,512]{2,1,0:T(2,128)(2,1)} %copy.21) | data formatting | bytes 2097152 | tf_op jit(solution)/shard_map/reshape | solution.py:101
  71.1 5.3 %convolution_convert_fusion = bf16[1024,512]{1,0:T(8,128)(2,1)} fusion(bf16[1024,512]{1,0:T(8,128)(2,1)} %reshape.59, bf16[1,1024,512]{2,1,0:T(8,128)(2,1)} %param.13, bf16[1,512,1024]{2,1,0:T(8,128)(2,1)} %param.12), kind=kOutput, calls=%fused_computation.34 | convolution fusion | flops 2157445120 | bytes 4194304 | tf_op jit(solution)/shard_map/dot_general | solution.py:105
  76.4 2.3 %reshape.60 = bf16[512,2,512]{2,1,0:T(2,128)(2,1)} reshape(bf16[1024,512]{1,0:T(8,128)(2,1)} %convolution_convert_fusion) | data formatting | bytes 2097152 | tf_op jit(solution)/shard_map/reshape | solution.py:107
  78.6 2.4 %copy.22 = bf16[512,2,512]{2,0,1:T(8,128)(2,1)} copy(bf16[512,2,512]{2,1,0:T(2,128)(2,1)} %reshape.60) | data formatting | bytes 2097152 | tf_op jit(solution)/shard_map/reshape | solution.py:107
  81.0 20.6 %all-reduce.2.cloned.1.call-done = bf16[512,2,512]{2,0,1:T(8,128)(2,1)} async-done(((bf16[512,2,512]{2,0,1:T(8,128)(2,1)}), bf16[512,2,512]{2,0,1:T(8,128)(2,1)}) %all-reduce.2.cloned.1.call-update) | async-done | bytes 1048592 | tf_op jit(solution)/shard_map/psum | solution.py:106
  101.6 1.6 %add_convert_fusion = bf16[512,2,512]{2,0,1:T(8,128)(2,1)S(1)} fusion(f32[512,2,512]{2,0,1:T(8,128)S(1)} %get-tuple-element.6, bf16[512,2,512]{2,0,1:T(8,128)(2,1)} %all-reduce.2.cloned.1.call-done), kind=kLoop, calls=%fused_computation.25 | loop fusion | flops 1572864 | bytes 4194304 | tf_op jit(solution)/shard_map/convert_element_type | solution.py:108
  103.2 2.0 %copy.23 = bf16[512,2,512]{2,1,0:T(2,128)(2,1)} copy(bf16[512,2,512]{2,0,1:T(8,128)(2,1)S(1)} %add_convert_fusion) | data formatting | bytes 2097152 | tf_op jit(solution)/shard_map/convert_element_type | solution.py:108
  (26 shorter events, 3.1 us)
Async XLA Ops:
  6.5 2.4 %copy-start = (bf16[2,1024,256]{2,1,0:T(8,128)(2,1)S(1)}, bf16[2,1024,256]{2,1,0:T(8,128)(2,1)}, u32[]{:S(2)}) copy-start(bf16[2,1024,256]{2,1,0:T(8,128)(2,1)} %param.7) | copy-start | bytes 3145732
  6.5 95.0 %all-reduce.2.cloned.1.call-start = ((), (), s32[]{:S(2)}) async-start(), calls=%async_computation | async-start | bytes 2097152 | tf_op jit(solution)/shard_map/psum | solution.py:106
  10.2 8.0 %collective-permute-start = (bf16[1,384,256]{2,1,0:T(8,128)(2,1)S(1)}, bf16[1,384,256]{2,1,0:T(8,128)(2,1)S(1)}, u32[]{:S(2)}, u32[]{:S(2)}) collective-permute-start(bf16[1,384,256]{2,1,0:T(8,128)(2,1)S(1)} %bitcast.50), channel_id=1, source_target_pairs={{0,4},{4,0},{8,12},{12,8},{1,5},{5,1},{9,13},{13,9},{2,6},{6,2},{1... | collective-permute-start | bytes 589832 | tf_op jit(solution)/shard_map/ppermute | solution.py:21
  18.3 19.7 %collective-permute-start.1 = (bf16[2,384,256]{2,1,0:T(8,128)(2,1)S(1)}, bf16[2,384,256]{2,1,0:T(8,128)(2,1)S(1)}, u32[]{:S(2)}, u32[]{:S(2)}) collective-permute-start(bf16[2,384,256]{2,1,0:T(8,128)(2,1)S(1)} %get-tuple-element.10), channel_id=1, source_target_pairs={{0,8},{4,12},{8,0},{12,4},{1,9},{5,13},{9,1},{13,5},{2,10},{6,14},... | collective-permute-start | bytes 1179656 | tf_op jit(solution)/shard_map/ppermute | solution.py:21
  45.4 1.0 copy-start.2
  47.3 4.3 %copy-start.1 = (f32[1,3,512]{2,0,1:T(1,128)S(1)}, f32[1,3,512]{2,0,1:T(1,128)}, u32[]{:S(2)}) copy-start(f32[1,3,512]{2,0,1:T(1,128)} %param.11) | copy-start | bytes 18436
  47.6 13.8 %collective-permute-start.2 = (bf16[512,1,512]{2,0,1:T(8,128)(2,1)S(1)}, bf16[512,1,512]{2,0,1:T(8,128)(2,1)S(1)}, u32[]{:S(2)}, u32[]{:S(2)}) collective-permute-start(bf16[512,1,512]{2,0,1:T(8,128)(2,1)S(1)} %get-tuple-element.7), channel_id=1, source_target_pairs={{0,4},{4,8},{8,12},{1,5},{5,9},{9,13},{2,6},{6,10},{10,14},{3,7},{... | collective-permute-start | bytes 1572872 | tf_op jit(solution)/shard_map/ppermute | solution.py:36
  50.1 15.5 %collective-permute-start.3 = (bf16[512,1,512]{2,0,1:T(8,128)(2,1)S(1)}, bf16[512,1,512]{2,0,1:T(8,128)(2,1)S(1)}, u32[]{:S(2)}, u32[]{:S(2)}) collective-permute-start(bf16[512,1,512]{2,0,1:T(8,128)(2,1)S(1)} %get-tuple-element.8), channel_id=1, source_target_pairs={{4,0},{8,4},{12,8},{5,1},{9,5},{13,9},{6,2},{10,6},{14,10},{7,3},{... | collective-permute-start | bytes 1572872 | tf_op jit(solution)/shard_map/ppermute | solution.py:38
Sparse Core Ops, SparseCore 0:
  81.1 20.4 all-reduce.1
